TPU v7x, 32 devices: a whole 2x2x4 slice. The times are simulated.
32 devices in a mesh: head: 8 (over z, x), seq: 4 (over y, core).
Axes of the slice: x: 2, y: 2, z: 4, core: 2. Of those that a mesh axis runs over, the one named last changes fastest.
Arguments:
- queries: bfloat16 [4, 1024, 4096], P('seq', 'head'), may hold values from -8 to 8
- key_row_matrix: bfloat16 [4, 1024, 1024], P('seq', 'head'), may hold values from -8 to 8
- values: bfloat16 [4, 1024, 1024], P('seq', 'head'), may hold values from -6 to 6
- verticals: int32 [32, 6], replicated, may hold values from 0 to 31, as said below
- slashes: int32 [32, 3], replicated, may hold values from 1 to 7, as said below
- counts: int32 [32, 2], replicated, may hold values from 0 to 6, as said below
Outputs:
- context: bfloat16 [4, 1024, 4096], P('seq', 'head')
Inputs may be any that keep to these rules, and one draw needn't show every extreme that they name: `verticals`: each row holds 6 different key blocks. `slashes`: each row holds 3 different block offsets. `counts`: column 0 is at least 1; some head uses all 6 and all 3 slots.
All inputs are finite; a program needn't handle non-finite values.
Results may differ from a plain program's by a relative error of at most 0.0037.
Values may be sent and summed in bfloat16 or wider, within the bound.
A program may use at most 64 MiB of HBM per device.

v0:
```python
import functools
import math

import jax
import jax.numpy as jnp
from jax import lax
from jax.experimental import pallas as pl
from jax.experimental.pallas import tpu as pltpu
from jax.sharding import PartitionSpec as P

QUERY_HEADS = 32
KEY_VALUE_HEADS = 8
HEAD_WIDTH = 128
BLOCK_TOKENS = 128
GROUP = KEY_VALUE_HEADS
SHARED = QUERY_HEADS // KEY_VALUE_HEADS
WIDE = SHARED * HEAD_WIDTH
ORDER = (4, 2, 6, 5, 3, 7, 1)
MESH = pl.DeviceIdType.MESH
VMEM = pl.BlockSpec(memory_space=pltpu.VMEM)
SMEM = pl.BlockSpec(memory_space=pltpu.SMEM)


def flipped(member, bits):
    parts = (member % 2, (member // 2) % 2, member // 4)
    return sum(((part + ((bits >> k) & 1)) % 2) * (1 << k) for k, part in enumerate(parts))


def place():
    seqs = lax.axis_size("seq")
    number = lax.axis_index("head") * seqs + lax.axis_index("seq")
    return seqs, number, number // GROUP, number % GROUP


def greet(barrier, seqs, number):
    pl.semaphore_signal(
        barrier, inc=1, device_id=(number // seqs, number % seqs), device_id_type=MESH
    )


def spread_kernel(
    groups, q_in, k_in, v_in, q_out, kv_out, own, kv_send, kv_got, q_send, q_got, z_send, z_got
):
    seqs, me, plane, member = place()
    base = plane * GROUP
    has_above = plane < groups - 1
    has_below = plane > 0
    barrier = pltpu.get_barrier_semaphore()
    for bits in ORDER:
        greet(barrier, seqs, base + flipped(member, bits))

    @pl.when(has_above)
    def _():
        greet(barrier, seqs, me + GROUP)

    @pl.when(has_below)
    def _():
        greet(barrier, seqs, me - GROUP)

    def narrow(ref, to):
        return ref.at[:, pl.ds(pl.multiple_of(to * HEAD_WIDTH, HEAD_WIDTH), HEAD_WIDTH)]

    def wide(ref, to):
        return ref.at[:, pl.ds(pl.multiple_of(to * WIDE, WIDE), WIDE)]

    stay = [
        pltpu.make_async_copy(narrow(k_in, member), kv_out.at[me, 0], own.at[0]),
        pltpu.make_async_copy(narrow(v_in, member), kv_out.at[me, 1], own.at[1]),
        pltpu.make_async_copy(wide(q_in, member), q_out.at[member], own.at[2]),
    ]
    for copy in stay:
        copy.start()
    pl.semaphore_wait(
        barrier, GROUP - 1 + jnp.where(has_above, 1, 0) + jnp.where(has_below, 1, 0)
    )

    def remote(src, dst, send, got, to):
        return pltpu.make_async_remote_copy(
            src_ref=src,
            dst_ref=dst,
            send_sem=send,
            recv_sem=got,
            device_id=(to // seqs, to % seqs),
            device_id_type=MESH,
        )

    kv_copies, q_copies = [], []
    for bits in ORDER:
        to = flipped(member, bits)
        for which, ref in enumerate((k_in, v_in)):
            kv_copies.append(
                remote(
                    narrow(ref, to),
                    kv_out.at[me, which],
                    kv_send.at[which, bits],
                    kv_got.at[which, bits],
                    base + to,
                )
            )
            kv_copies[-1].start()
    def up(block):
        return remote(
            kv_out.at[block], kv_out.at[block], z_send.at[0, block], z_got.at[block], me + GROUP
        )

    def down(block):
        return remote(
            kv_out.at[block], kv_out.at[block], z_send.at[1, block], z_got.at[block], me - GROUP
        )

    def pass_on(block, upward, downward):
        if upward:

            @pl.when(has_above)
            def _():
                up(block).start()

        if downward:

            @pl.when(has_below)
            def _():
                down(block).start()

    stay[0].wait()
    stay[1].wait()
    pass_on(me, True, True)
    for at, bits in enumerate(ORDER):
        kv_copies[2 * at].wait_recv()
        kv_copies[2 * at + 1].wait_recv()
        pass_on(base + flipped(member, bits), True, True)
    for bits in ORDER:
        to = flipped(member, bits)
        q_copies.append(
            remote(wide(q_in, to), q_out.at[member], q_send.at[bits], q_got.at[bits], base + to)
        )
        q_copies[-1].start()

    def far_step(step, carry):
        for bits in (0,) + ORDER:
            other = flipped(member, bits)
            lower = (plane - step) * GROUP + other
            upper = (plane + step) * GROUP + other

            @pl.when(plane - step >= 0)
            def _():
                up(lower).wait_recv()
                pass_on(lower, True, False)

            @pl.when(plane + step < groups)
            def _():
                down(upper).wait_recv()
                pass_on(upper, False, True)

        return carry

    lax.fori_loop(1, groups, far_step, 0)
    stay[2].wait()
    for copy in kv_copies:
        copy.wait_send()
    for copy in q_copies:
        copy.wait()

    def sent_step(step, carry):
        for other in range(GROUP):
            block = step * GROUP + other

            @pl.when(has_above & (step <= plane))
            def _():
                up(block).wait_send()

            @pl.when(has_below & (step >= plane))
            def _():
                down(block).wait_send()

        return carry

    lax.fori_loop(0, groups, sent_step, 0)


def spread(queries, keys, values, groups):
    count = groups * GROUP
    rows = queries.shape[0]
    return pl.pallas_call(
        functools.partial(spread_kernel, groups),
        name="spread",
        out_shape=(
            jax.ShapeDtypeStruct((GROUP, rows, WIDE), jnp.bfloat16),
            jax.ShapeDtypeStruct((count, 2, rows, HEAD_WIDTH), jnp.bfloat16),
        ),
        in_specs=[VMEM] * 3,
        out_specs=(VMEM, VMEM),
        scratch_shapes=[
            pltpu.SemaphoreType.DMA((3,)),
            pltpu.SemaphoreType.DMA((2, GROUP)),
            pltpu.SemaphoreType.DMA((2, GROUP)),
            pltpu.SemaphoreType.DMA((GROUP,)),
            pltpu.SemaphoreType.DMA((GROUP,)),
            pltpu.SemaphoreType.DMA((2, count)),
            pltpu.SemaphoreType.DMA((count,)),
        ],
        compiler_params=pltpu.CompilerParams(collective_id=0, has_side_effects=True),
    )(queries, keys, values)


def attend_kernel(verticals, slashes, counts, q, kv, out, scores, top, total, mixed):
    heads = lax.axis_size("head")
    seqs, me, plane, member = place()
    base = plane * GROUP
    slash_slots = slashes.shape[0]
    factor = math.log2(math.e) / math.sqrt(HEAD_WIDTH)
    rows = lax.broadcasted_iota(jnp.int32, (BLOCK_TOKENS, BLOCK_TOKENS), 0)
    cols = lax.broadcasted_iota(jnp.int32, (BLOCK_TOKENS, BLOCK_TOKENS), 1)
    causal = rows >= cols
    block_ids = [
        ((base + t) % seqs) * heads + (base + t) // seqs for t in range(GROUP)
    ]

    def holder(block):
        return (block % heads) * seqs + block // heads

    def product(left, right, dims):
        return lax.dot_general(left, right, (dims, ((), ())), preferred_element_type=jnp.float32)

    def one_head(j, carry):
        head = member * SHARED + j
        columns = pl.ds(pl.multiple_of(j * HEAD_WIDTH, HEAD_WIDTH), HEAD_WIDTH)
        n_slash = counts[1, head]
        n_column = counts[0, head]

        def keep(slot, t, key, active):
            found = product(q[t, :, columns], key, ((1,), (1,)))
            found = jnp.where(active, found, -jnp.inf)
            scores[slot, t] = found
            top[t] = jnp.maximum(top[t], found)

        for t in range(GROUP):
            found = product(q[t, :, columns], kv[base + t, 0], ((1,), (1,)))
            found = jnp.where(causal, found, -jnp.inf)
            scores[0, t] = found
            top[t] = found

        def slash_scores(slot, carry):
            offset = slashes[slot, head]
            for t in range(GROUP):
                block = block_ids[t] - offset
                keep(1 + slot, t, kv[holder(jnp.maximum(block, 0)), 0], block >= 0)
            return carry

        def column_scores(slot, carry):
            column = verticals[slot, head]
            key = kv[holder(column), 0]
            for t in range(GROUP):
                active = column < block_ids[t]
                for s in range(slash_slots):
                    repeated = (block_ids[t] - column == slashes[s, head]) & (s < n_slash)
                    active = active & jnp.logical_not(repeated)
                keep(1 + n_slash + slot, t, key, active)
            return carry

        lax.fori_loop(0, n_slash, slash_scores, 0)
        lax.fori_loop(0, n_column, column_scores, 0)

        def weigh(slot, t, first, value):
            weights = jnp.exp2((scores[slot, t] - top[t]) * factor)
            part = product(weights.astype(jnp.bfloat16), value, ((1,), (0,)))
            if first:
                total[t] = weights
                mixed[t] = part
            else:
                total[t] = total[t] + weights
                mixed[t] = mixed[t] + part

        for t in range(GROUP):
            top[t] = jnp.broadcast_to(jnp.max(top[t], axis=1, keepdims=True), top.shape[1:])
        for t in range(GROUP):
            weigh(0, t, True, kv[base + t, 1])

        def slash_mix(slot, carry):
            offset = slashes[slot, head]
            for t in range(GROUP):
                block = jnp.maximum(block_ids[t] - offset, 0)
                weigh(1 + slot, t, False, kv[holder(block), 1])
            return carry

        def column_mix(slot, carry):
            value = kv[holder(verticals[slot, head]), 1]
            for t in range(GROUP):
                weigh(1 + n_slash + slot, t, False, value)
            return carry

        lax.fori_loop(0, n_slash, slash_mix, 0)
        lax.fori_loop(0, n_column, column_mix, 0)
        for t in range(GROUP):
            sums = jnp.sum(total[t], axis=1, keepdims=True)
            out[t, :, columns] = (mixed[t] / sums).astype(out.dtype)
        return carry

    lax.fori_loop(0, SHARED, one_head, 0)


def attend(verticals, slashes, counts, queries, pairs):
    slots = 1 + verticals.shape[0] + slashes.shape[0]
    tile = (BLOCK_TOKENS, BLOCK_TOKENS)
    return pl.pallas_call(
        attend_kernel,
        name="attend",
        out_shape=jax.ShapeDtypeStruct(queries.shape, jnp.bfloat16),
        in_specs=[SMEM] * 3 + [VMEM] * 2,
        out_specs=VMEM,
        scratch_shapes=[
            pltpu.VMEM((slots, GROUP) + tile, jnp.float32),
            pltpu.VMEM((GROUP,) + tile, jnp.float32),
            pltpu.VMEM((GROUP,) + tile, jnp.float32),
            pltpu.VMEM((GROUP,) + tile, jnp.float32),
        ],
    )(verticals, slashes, counts, queries, pairs)


def collect_kernel(o_in, out, own, send, got):
    seqs, me, plane, member = place()
    base = plane * GROUP
    barrier = pltpu.get_barrier_semaphore()
    for bits in ORDER:
        greet(barrier, seqs, base + flipped(member, bits))
    mine = out.at[:, pl.ds(pl.multiple_of(member * WIDE, WIDE), WIDE)]
    stay = pltpu.make_async_copy(o_in.at[member], mine, own)
    stay.start()
    pl.semaphore_wait(barrier, GROUP - 1)
    copies = []
    for bits in ORDER:
        to = flipped(member, bits)
        copies.append(
            pltpu.make_async_remote_copy(
                src_ref=o_in.at[to],
                dst_ref=mine,
                send_sem=send.at[bits],
                recv_sem=got.at[bits],
                device_id=((base + to) // seqs, (base + to) % seqs),
                device_id_type=MESH,
            )
        )
        copies[-1].start()
    stay.wait()
    for copy in copies:
        copy.wait()


def collect(outputs):
    rows = outputs.shape[1]
    return pl.pallas_call(
        collect_kernel,
        name="collect",
        out_shape=jax.ShapeDtypeStruct((rows, GROUP * WIDE), jnp.bfloat16),
        in_specs=[VMEM],
        out_specs=VMEM,
        scratch_shapes=[
            pltpu.SemaphoreType.DMA,
            pltpu.SemaphoreType.DMA((GROUP,)),
            pltpu.SemaphoreType.DMA((GROUP,)),
        ],
        compiler_params=pltpu.CompilerParams(collective_id=1, has_side_effects=True),
    )(outputs)


def shards(queries, key_row_matrix, values, verticals, slashes, counts):
    assert queries.shape[1] == BLOCK_TOKENS
    groups = lax.axis_size("head") * lax.axis_size("seq") // GROUP
    own, pairs = spread(queries[0], key_row_matrix[0], values[0], groups)
    outputs = attend(verticals.T, slashes.T, counts.T, own, pairs)
    return collect(outputs)[None]


def solution(mesh):
    in_specs = (
        P("seq", "head", None),
        P("seq", "head", None),
        P("seq", "head", None),
        P(),
        P(),
        P(),
    )
    out_specs = P("seq", "head", None)
    return jax.shard_map(shards, mesh=mesh, in_specs=in_specs, out_specs=out_specs, check_vma=False)
```

profile of v0, /device:TPU:5, one launch (start us, length us, event | category | flops | bytes accessed | tf_op | source)
XLA Modules:
  0.0 85.6 jit_solution(12356233534674596649)
XLA Ops:
  0.0 43.8 %spread.1 = (bf16[8,128,512]{2,1,0:T(8,128)(2,1)}, bf16[32,2,128,128]{3,2,1,0:T(8,128)(2,1)}) custom-call(bf16[128,4096]{1,0:T(8,128)(2,1)} %bitcast.8, bf16[128,1024]{1,0:T(8,128)(2,1)} %bitcast.9, bf16[128,1024]{1,0:T(8,128)(2,1)} %bitcast.10), custom_call_target="tpu_custom_call" | custom-call | tf_op jit(solution)/shard_map/spread/pallas_call | solution.py:183
  43.8 22.6 %attend.1.o_in = bf16[8,128,512]{2,1,0:T(8,128)(2,1)} custom-call(s32[6,32]{1,0:T(8,128)} %bitcast.11, s32[3,32]{1,0:T(4,128)} %bitcast.12, s32[2,32]{1,0:T(2,128)} %bitcast.13, bf16[8,128,512]{2,1,0:T(8,128)(2,1)} %get-tuple-element.7.q, bf16[32,2,128,128]{3,2,1,0:T(8,128)(2,1)} %get-tuple-element.8.kv), custom_call_target="tpu_custom_call" | custom-call | tf_op jit(solution)/shard_map/attend/pallas_call | solution.py:304
  66.3 17.0 %collect.1 = bf16[128,4096]{1,0:T(8,128)(2,1)} custom-call(bf16[8,128,512]{2,1,0:T(8,128)(2,1)} %attend.1.o_in), custom_call_target="tpu_custom_call" | custom-call | tf_op jit(solution)/shard_map/collect/pallas_call | solution.py:350
  83.3 2.3 %copy.8 = bf16[1,128,4096]{2,1,0:T(8,128)(2,1)} copy(bf16[1,128,4096]{2,1,0:T(8,128)(2,1)} %bitcast.7) | data formatting | bytes 2097152
where the time goes:
time: 85.5 us; the launch traced here: 85.6 us
  Pallas kernels  83.3 us (97%)
  local copies, waits for them, and re-layouts  2.29 us (3%)
    pallas_call x1, Pallas kernels, spread(): pl.pallas_call(functools.partial(spread_kernel, groups), name='spread', o...  43.8 us
    pallas_call x1, Pallas kernels, attend(): pl.pallas_call(attend_kernel, name='attend', out_shape=jax.ShapeDtypeStru...  22.6 us
    pallas_call x1, Pallas kernels, collect(): pl.pallas_call(collect_kernel, name='collect', out_shape=jax.ShapeDtypeSt...  17 us
    unnamed x1, local copies, waits for them, and re-layouts  2.29 us

commit v1 on v0

v1 whole, which is shorter than its diff:
```python
import functools
import math

import jax
import jax.numpy as jnp
from jax import lax
from jax.experimental import pallas as pl
from jax.experimental.pallas import tpu as pltpu
from jax.sharding import PartitionSpec as P

QUERY_HEADS = 32
KEY_VALUE_HEADS = 8
HEAD_WIDTH = 128
BLOCK_TOKENS = 128
GROUP = KEY_VALUE_HEADS
SHARED = QUERY_HEADS // KEY_VALUE_HEADS
WIDE = SHARED * HEAD_WIDTH
ORDER = (4, 2, 6, 5, 3, 7, 1)
MESH = pl.DeviceIdType.MESH
ANY = pl.BlockSpec(memory_space=pl.ANY)
VMEM_BYTES = 62 * 1024 * 1024
SMEM = pl.BlockSpec(memory_space=pltpu.SMEM)


def flipped(member, bits):
    parts = (member % 2, (member // 2) % 2, member // 4)
    return sum(((part + ((bits >> k) & 1)) % 2) * (1 << k) for k, part in enumerate(parts))


def flipped_by(member, bits):
    total = 0
    for size in (1, 2, 4):
        total += lax.rem(lax.div(member, size) + lax.div(bits, size), 2) * size
    return total


def place():
    seqs = lax.axis_size("seq")
    number = lax.axis_index("head") * seqs + lax.axis_index("seq")
    return seqs, number, number // GROUP, number % GROUP


def greet(barrier, seqs, number):
    pl.semaphore_signal(
        barrier, inc=1, device_id=(number // seqs, number % seqs), device_id_type=MESH
    )


def kernel(
    groups, verticals, slashes, counts, q_in, k_in, v_in, out, queries, keys, values, scores, top,
    results, own, kv_send, kv_got, q_send, q_got, k_pass, k_got, v_pass, v_got, o_send, o_got
):
    heads = lax.axis_size("head")
    seqs, me, plane, member = place()
    base = plane * GROUP
    has_above = plane < groups - 1
    has_below = plane > 0
    barrier = pltpu.get_barrier_semaphore()
    for bits in ORDER:
        greet(barrier, seqs, base + flipped(member, bits))

    @pl.when(has_above)
    def _():
        greet(barrier, seqs, me + GROUP)

    @pl.when(has_below)
    def _():
        greet(barrier, seqs, me - GROUP)

    def narrow(ref, to):
        return ref.at[:, pl.ds(pl.multiple_of(to * HEAD_WIDTH, HEAD_WIDTH), HEAD_WIDTH)]

    def wide(ref, to):
        return ref.at[:, pl.ds(pl.multiple_of(to * WIDE, WIDE), WIDE)]

    def remote(src, dst, send, got, to):
        return pltpu.make_async_remote_copy(
            src_ref=src,
            dst_ref=dst,
            send_sem=send,
            recv_sem=got,
            device_id=(to // seqs, to % seqs),
            device_id_type=MESH,
        )

    stay = [
        pltpu.make_async_copy(narrow(k_in, member), keys.at[me], own.at[0]),
        pltpu.make_async_copy(narrow(v_in, member), values.at[me], own.at[1]),
        pltpu.make_async_copy(wide(q_in, member), queries.at[member], own.at[2]),
    ]
    for copy in stay:
        copy.start()
    pl.semaphore_wait(
        barrier, GROUP - 1 + jnp.where(has_above, 1, 0) + jnp.where(has_below, 1, 0)
    )
    near = ([], [], [])
    for which, (ref, kept) in enumerate(((k_in, keys), (v_in, values))):
        for bits in ORDER:
            to = flipped(member, bits)
            near[which].append(
                remote(
                    narrow(ref, to),
                    kept.at[me],
                    kv_send.at[which, bits],
                    kv_got.at[which, bits],
                    base + to,
                )
            )
            near[which][-1].start()
    for bits in ORDER:
        to = flipped(member, bits)
        near[2].append(
            remote(wide(q_in, to), queries.at[member], q_send.at[bits], q_got.at[bits], base + to)
        )
        near[2][-1].start()

    def relay(ref, send, got):
        def up(block):
            return remote(ref.at[block], ref.at[block], send.at[0, block], got.at[block], me + GROUP)

        def down(block):
            return remote(ref.at[block], ref.at[block], send.at[1, block], got.at[block], me - GROUP)

        def pass_on(block, upward, downward):
            if upward:

                @pl.when(has_above)
                def _():
                    up(block).start()

            if downward:

                @pl.when(has_below)
                def _():
                    down(block).start()

        def far(step, bits):
            other = flipped_by(member, bits)
            lower = (plane - step) * GROUP + other
            upper = (plane + step) * GROUP + other

            @pl.when(plane - step >= 0)
            def _():
                up(lower).wait_recv()
                pass_on(lower, True, False)

            @pl.when(plane + step < groups)
            def _():
                down(upper).wait_recv()
                pass_on(upper, False, True)

        def sent(step, carry):
            for other in range(GROUP):
                block = step * GROUP + other

                @pl.when(has_above & (step <= plane))
                def _():
                    up(block).wait_send()

                @pl.when(has_below & (step >= plane))
                def _():
                    down(block).wait_send()

            return carry

        return pass_on, far, sent

    def start_relay(which, pass_on):
        stay[which].wait()
        pass_on(me, True, True)
        for at, bits in enumerate(ORDER):
            near[which][at].wait_recv()
            pass_on(base + flipped(member, bits), True, True)

    k_on, k_far, k_sent = relay(keys, k_pass, k_got)
    v_on, v_far, v_sent = relay(values, v_pass, v_got)

    slash_slots = slashes.shape[0]
    column_slots = verticals.shape[0]
    factor = math.log2(math.e) / math.sqrt(HEAD_WIDTH)
    units = SHARED * GROUP
    steps = (groups - 1) * GROUP

    def holder(block):
        return lax.rem(block, heads) * seqs + lax.div(block, heads)

    def product(left, right, dims):
        return lax.dot_general(left, right, (dims, ((), ())), preferred_element_type=jnp.float32)

    def unit_facts(unit):
        head = member * SHARED + unit // GROUP
        number = base + unit % GROUP
        return head, number, lax.rem(number, seqs) * heads + lax.div(number, seqs)

    def score_unit(unit):
        head, number, block = unit_facts(unit)
        at = pl.multiple_of(unit // GROUP * HEAD_WIDTH, HEAD_WIDTH)
        query = queries[unit % GROUP, :, pl.ds(at, HEAD_WIDTH)]
        rows = lax.broadcasted_iota(jnp.int32, (BLOCK_TOKENS, BLOCK_TOKENS), 0)
        cols = lax.broadcasted_iota(jnp.int32, (BLOCK_TOKENS, BLOCK_TOKENS), 1)
        best = product(query, keys[number], ((1,), (1,)))
        best = jnp.where(rows >= cols, best, -jnp.inf)
        scores[unit, 0] = best
        for slot in range(slash_slots):
            other = block - slashes[slot, head]
            active = (other >= 0) & (slot < counts[1, head])
            found = product(query, keys[holder(jnp.maximum(other, 0))], ((1,), (1,)))
            found = jnp.where(active, found, -jnp.inf)
            scores[unit, 1 + slot] = found
            best = jnp.maximum(best, found)
        for slot in range(column_slots):
            column = verticals[slot, head]
            active = (column < block) & (slot < counts[0, head])
            for s in range(slash_slots):
                repeated = (block - column == slashes[s, head]) & (s < counts[1, head])
                active = active & jnp.logical_not(repeated)
            found = product(query, keys[holder(column)], ((1,), (1,)))
            found = jnp.where(active, found, -jnp.inf)
            scores[unit, 1 + slash_slots + slot] = found
            best = jnp.maximum(best, found)
        top[unit] = jnp.broadcast_to(jnp.max(best, axis=1, keepdims=True), top.shape[1:])

    def mix_unit(unit):
        head, number, block = unit_facts(unit)
        places = [number]
        for slot in range(slash_slots):
            places.append(holder(jnp.maximum(block - slashes[slot, head], 0)))
        for slot in range(column_slots):
            places.append(holder(verticals[slot, head]))
        total = mixed = None
        for slot, at in enumerate(places):
            weights = jnp.exp2((scores[unit, slot] - top[unit]) * factor)
            part = product(weights.astype(jnp.bfloat16), values[at], ((1,), (0,)))
            total = weights if total is None else total + weights
            mixed = part if mixed is None else mixed + part
        mixed = mixed / jnp.sum(total, axis=1, keepdims=True)
        results[unit] = mixed.astype(jnp.bfloat16)

    start_relay(0, k_on)

    def k_step(n, carry):
        k_far(n // GROUP + 1, n % GROUP)
        return carry

    lax.fori_loop(0, steps, k_step, 0)
    start_relay(1, v_on)
    stay[2].wait()
    for copy in near[2]:
        copy.wait_recv()
    lead = max(units - steps, 0)

    def lead_step(n, carry):
        score_unit(n)
        return carry

    def v_step(n, carry):
        if lead + steps == units:
            score_unit(lead + n)
        else:

            @pl.when(n < units)
            def _():
                score_unit(n)

        v_far(n // GROUP + 1, n % GROUP)
        return carry

    lax.fori_loop(0, lead, lead_step, 0)
    lax.fori_loop(0, steps, v_step, 0)

    def unit_of(n):
        return (n // GROUP) * GROUP + flipped_by(member, n % GROUP)

    def column_of(ref, j):
        at = pl.multiple_of((member * SHARED + j) * HEAD_WIDTH, HEAD_WIDTH)
        return ref.at[:, pl.ds(at, HEAD_WIDTH)]

    def give(n):
        j, bits = n // GROUP, n % GROUP
        unit = unit_of(n)
        return remote(
            results.at[unit],
            column_of(out, j),
            o_send.at[j, bits],
            o_got.at[j, bits],
            base + flipped_by(member, bits),
        )

    def take(j, bits):
        owner = flipped_by(member, bits)
        at = pl.multiple_of((owner * SHARED + j) * HEAD_WIDTH, HEAD_WIDTH)
        return remote(
            results.at[j * GROUP],
            out.at[:, pl.ds(at, HEAD_WIDTH)],
            o_send.at[j, bits],
            o_got.at[j, bits],
            base + owner,
        )

    def hold(j):
        return pltpu.make_async_copy(
            results.at[j * GROUP + member], column_of(out, j), own.at[3 + j]
        )

    def hand_out(n):
        @pl.when(n % GROUP > 0)
        def _():
            give(n).start()

        @pl.when(n % GROUP == 0)
        def _():
            hold(n // GROUP).start()

    def mix_step(n, carry):
        mix_unit(unit_of(2 * n))
        mix_unit(unit_of(2 * n + 1))

        @pl.when(n > 0)
        def _():
            hand_out(2 * n - 2)
            hand_out(2 * n - 1)

        return carry

    lax.fori_loop(0, units // 2, mix_step, 0)
    hand_out(units - 2)
    hand_out(units - 1)
    for which in range(3):
        for copy in near[which]:
            copy.wait_send()
    lax.fori_loop(0, groups, k_sent, 0)
    lax.fori_loop(0, groups, v_sent, 0)
    for j in range(SHARED):
        hold(j).wait()
        for bits in ORDER:
            give(j * GROUP + bits).wait_send()
            take(j, bits).wait_recv()


def shards(queries, key_row_matrix, values, verticals, slashes, counts):
    rows, width = queries.shape[1:]
    assert rows == BLOCK_TOKENS
    groups = lax.axis_size("head") * lax.axis_size("seq") // GROUP
    count = groups * GROUP
    units = SHARED * GROUP
    slots = 1 + verticals.shape[1] + slashes.shape[1]
    block = (BLOCK_TOKENS, HEAD_WIDTH)
    out = pl.pallas_call(
        functools.partial(kernel, groups),
        name="block_sparse_attention",
        out_shape=jax.ShapeDtypeStruct((rows, width), jnp.bfloat16),
        in_specs=[SMEM] * 3 + [ANY] * 3,
        out_specs=ANY,
        scratch_shapes=[
            pltpu.VMEM((GROUP, rows, WIDE), jnp.bfloat16),
            pltpu.VMEM((count,) + block, jnp.bfloat16),
            pltpu.VMEM((count,) + block, jnp.bfloat16),
            pltpu.VMEM((units, slots, BLOCK_TOKENS, BLOCK_TOKENS), jnp.float32),
            pltpu.VMEM((units, BLOCK_TOKENS, BLOCK_TOKENS), jnp.float32),
            pltpu.VMEM((units,) + block, jnp.bfloat16),
            pltpu.SemaphoreType.DMA((3 + SHARED,)),
            pltpu.SemaphoreType.DMA((2, GROUP)),
            pltpu.SemaphoreType.DMA((2, GROUP)),
            pltpu.SemaphoreType.DMA((GROUP,)),
            pltpu.SemaphoreType.DMA((GROUP,)),
            pltpu.SemaphoreType.DMA((2, count)),
            pltpu.SemaphoreType.DMA((count,)),
            pltpu.SemaphoreType.DMA((2, count)),
            pltpu.SemaphoreType.DMA((count,)),
            pltpu.SemaphoreType.DMA((SHARED, GROUP)),
            pltpu.SemaphoreType.DMA((SHARED, GROUP)),
        ],
        compiler_params=pltpu.CompilerParams(
            collective_id=0, has_side_effects=True, vmem_limit_bytes=VMEM_BYTES
        ),
    )(verticals.T, slashes.T, counts.T, queries[0], key_row_matrix[0], values[0])
    return out[None]


def solution(mesh):
    in_specs = (
        P("seq", "head", None),
        P("seq", "head", None),
        P("seq", "head", None),
        P(),
        P(),
        P(),
    )
    out_specs = P("seq", "head", None)
    return jax.shard_map(shards, mesh=mesh, in_specs=in_specs, out_specs=out_specs, check_vma=False)
```

time: 85.5 us -> 63.1 us (0.74); the launches traced: 85.6 us -> 61.9 us
  Pallas kernels: 83.3 us -> 59.6 us
    pallas_call x3 -> x1, Pallas kernels: 83.3 us -> 59.6 us  [shards(): pl.pallas_call(functools.partial(kernel, groups), name='block_sparse_atte...]
where the time goes in v1:
time: 63.1 us; the launch traced here: 61.9 us
  Pallas kernels  59.6 us (94%)
  local copies, waits for them, and re-layouts  2.29 us (4%)
    pallas_call x1, Pallas kernels, shards(): pl.pallas_call(functools.partial(kernel, groups), name='block_sparse_atte...  59.6 us
    unnamed x1, local copies, waits for them, and re-layouts  2.29 us

profile of v1, /device:TPU:5, one launch (start us, length us, event | category | flops | bytes accessed | tf_op | source)
XLA Modules:
  0.0 61.9 jit_solution(15807281218213421131)
XLA Ops:
  0.0 59.6 %block_sparse_attention.1 = bf16[128,4096]{1,0:T(8,128)(2,1)} custom-call(s32[6,32]{1,0:T(8,128)} %bitcast.11, s32[3,32]{1,0:T(4,128)} %bitcast.12, s32[2,32]{1,0:T(2,128)} %bitcast.13, bf16[128,4096]{1,0:T(8,128)(2,1)} %bitcast.8, bf16[128,1024]{1,0:T(8,128)(2,1)} %bitcast.9, bf16[128,1024]{1,0:T(8,128)(2,1)} %bitcast.10), custom_call_target="tpu_custom_call" | custom-call | tf_op jit(solution)/shard_map/block_sparse_attention/pallas_call | solution.py:348
  59.6 2.3 %copy.8 = bf16[1,128,4096]{2,1,0:T(8,128)(2,1)} copy(bf16[1,128,4096]{2,1,0:T(8,128)(2,1)} %bitcast.7) | data formatting | bytes 2097152

commit v2 on v1

--- a/solution.py
+++ b/solution.py
@@ -27,11 +27,8 @@
     return sum(((part + ((bits >> k) & 1)) % 2) * (1 << k) for k, part in enumerate(parts))
 
 
-def flipped_by(member, bits):
-    total = 0
-    for size in (1, 2, 4):
-        total += lax.rem(lax.div(member, size) + lax.div(bits, size), 2) * size
-    return total
+def stages_for(seqs):
+    return seqs if GROUP % seqs == 0 else 1
 
 
 def place():
@@ -48,7 +45,7 @@
 
 def kernel(
     groups, verticals, slashes, counts, q_in, k_in, v_in, out, queries, keys, values, scores, top,
-    results, own, kv_send, kv_got, q_send, q_got, k_pass, k_got, v_pass, v_got, o_send, o_got
+    results, seen_keys, seen_values, own, kv_send, kv_got, q_send, q_got, k_pass, k_got, v_pass, v_got, o_send, o_got
 ):
     heads = lax.axis_size("head")
     seqs, me, plane, member = place()
@@ -93,26 +90,29 @@
     pl.semaphore_wait(
         barrier, GROUP - 1 + jnp.where(has_above, 1, 0) + jnp.where(has_below, 1, 0)
     )
-    near = ([], [], [])
-    for which, (ref, kept) in enumerate(((k_in, keys), (v_in, values))):
+    stages = stages_for(seqs)
+    each = GROUP // stages
+
+    def near_kv(which, owner, to):
+        ref, kept = ((k_in, keys), (v_in, values))[which]
+        return remote(
+            narrow(ref, to),
+            kept.at[base + owner],
+            kv_send.at[which, to],
+            kv_got.at[which, owner],
+            base + to,
+        )
+
+    def near_q(owner, to):
+        return remote(
+            wide(q_in, to), queries.at[owner], q_send.at[to], q_got.at[owner], base + to
+        )
+
+    for which in range(2):
         for bits in ORDER:
-            to = flipped(member, bits)
-            near[which].append(
-                remote(
-                    narrow(ref, to),
-                    kept.at[me],
-                    kv_send.at[which, bits],
-                    kv_got.at[which, bits],
-                    base + to,
-                )
-            )
-            near[which][-1].start()
+            near_kv(which, member, flipped(member, bits)).start()
     for bits in ORDER:
-        to = flipped(member, bits)
-        near[2].append(
-            remote(wide(q_in, to), queries.at[member], q_send.at[bits], q_got.at[bits], base + to)
-        )
-        near[2][-1].start()
+        near_q(member, flipped(member, bits)).start()
 
     def relay(ref, send, got):
         def up(block):
@@ -134,8 +134,7 @@
                 def _():
                     down(block).start()
 
-        def far(step, bits):
-            other = flipped_by(member, bits)
+        def far(step, other):
             lower = (plane - step) * GROUP + other
             upper = (plane + step) * GROUP + other
 
@@ -165,21 +164,43 @@
 
         return pass_on, far, sent
 
-    def start_relay(which, pass_on):
-        stay[which].wait()
-        pass_on(me, True, True)
-        for at, bits in enumerate(ORDER):
-            near[which][at].wait_recv()
-            pass_on(base + flipped(member, bits), True, True)
-
-    k_on, k_far, k_sent = relay(keys, k_pass, k_got)
-    v_on, v_far, v_sent = relay(values, v_pass, v_got)
+    k_relay = relay(keys, k_pass, k_got)
+    v_relay = relay(values, v_pass, v_got)
+
+    def set_off(phase):
+        stage, which = phase // 2, phase % 2
+        for i in range(each):
+            t = stage + stages * i
+
+            @pl.when(member == t)
+            def _():
+                stay[which].wait()
+
+            @pl.when(member != t)
+            def _():
+                near_kv(which, t, t).wait_recv()
+
+            (k_relay, v_relay)[which][0](base + t, True, True)
+
+    def note(phase):
+        if stages == 1:
+            return
+        stage, which = phase // 2, phase % 2
+        kept, seen = ((keys, seen_keys), (values, seen_values))[which]
+
+        def note_step(n, carry):
+            at = (n // each) * GROUP + stage + stages * (n % each)
+            seen[at] = kept[at]
+            return carry
+
+        lax.fori_loop(0, groups * each, note_step, 0)
 
     slash_slots = slashes.shape[0]
     column_slots = verticals.shape[0]
     factor = math.log2(math.e) / math.sqrt(HEAD_WIDTH)
-    units = SHARED * GROUP
-    steps = (groups - 1) * GROUP
+    key_blocks, value_blocks = (keys, values) if stages == 1 else (seen_keys, seen_values)
+    in_stage = SHARED * each
+    steps = (groups - 1) * each
 
     def holder(block):
         return lax.rem(block, heads) * seqs + lax.div(block, heads)
@@ -198,13 +219,13 @@
         query = queries[unit % GROUP, :, pl.ds(at, HEAD_WIDTH)]
         rows = lax.broadcasted_iota(jnp.int32, (BLOCK_TOKENS, BLOCK_TOKENS), 0)
         cols = lax.broadcasted_iota(jnp.int32, (BLOCK_TOKENS, BLOCK_TOKENS), 1)
-        best = product(query, keys[number], ((1,), (1,)))
+        best = product(query, key_blocks[number], ((1,), (1,)))
         best = jnp.where(rows >= cols, best, -jnp.inf)
         scores[unit, 0] = best
         for slot in range(slash_slots):
             other = block - slashes[slot, head]
             active = (other >= 0) & (slot < counts[1, head])
-            found = product(query, keys[holder(jnp.maximum(other, 0))], ((1,), (1,)))
+            found = product(query, key_blocks[holder(jnp.maximum(other, 0))], ((1,), (1,)))
             found = jnp.where(active, found, -jnp.inf)
             scores[unit, 1 + slot] = found
             best = jnp.maximum(best, found)
@@ -214,7 +235,7 @@
             for s in range(slash_slots):
                 repeated = (block - column == slashes[s, head]) & (s < counts[1, head])
                 active = active & jnp.logical_not(repeated)
-            found = product(query, keys[holder(column)], ((1,), (1,)))
+            found = product(query, key_blocks[holder(jnp.minimum(column, block))], ((1,), (1,)))
             found = jnp.where(active, found, -jnp.inf)
             scores[unit, 1 + slash_slots + slot] = found
             best = jnp.maximum(best, found)
@@ -226,115 +247,152 @@
         for slot in range(slash_slots):
             places.append(holder(jnp.maximum(block - slashes[slot, head], 0)))
         for slot in range(column_slots):
-            places.append(holder(verticals[slot, head]))
+            places.append(holder(jnp.minimum(verticals[slot, head], block)))
         total = mixed = None
         for slot, at in enumerate(places):
             weights = jnp.exp2((scores[unit, slot] - top[unit]) * factor)
-            part = product(weights.astype(jnp.bfloat16), values[at], ((1,), (0,)))
+            part = product(weights.astype(jnp.bfloat16), value_blocks[at], ((1,), (0,)))
             total = weights if total is None else total + weights
             mixed = part if mixed is None else mixed + part
         mixed = mixed / jnp.sum(total, axis=1, keepdims=True)
         results[unit] = mixed.astype(jnp.bfloat16)
 
-    start_relay(0, k_on)
-
-    def k_step(n, carry):
-        k_far(n // GROUP + 1, n % GROUP)
-        return carry
-
-    lax.fori_loop(0, steps, k_step, 0)
-    start_relay(1, v_on)
-    stay[2].wait()
-    for copy in near[2]:
-        copy.wait_recv()
-    lead = max(units - steps, 0)
-
-    def lead_step(n, carry):
-        score_unit(n)
-        return carry
-
-    def v_step(n, carry):
-        if lead + steps == units:
-            score_unit(lead + n)
-        else:
-
-            @pl.when(n < units)
-            def _():
-                score_unit(n)
-
-        v_far(n // GROUP + 1, n % GROUP)
-        return carry
-
-    lax.fori_loop(0, lead, lead_step, 0)
-    lax.fori_loop(0, steps, v_step, 0)
-
-    def unit_of(n):
-        return (n // GROUP) * GROUP + flipped_by(member, n % GROUP)
-
-    def column_of(ref, j):
-        at = pl.multiple_of((member * SHARED + j) * HEAD_WIDTH, HEAD_WIDTH)
+    def unit_in(stage, n):
+        return n // each * GROUP + stage + stages * (n % each)
+
+    def column_of(ref, owner, j):
+        at = pl.multiple_of((owner * SHARED + j) * HEAD_WIDTH, HEAD_WIDTH)
         return ref.at[:, pl.ds(at, HEAD_WIDTH)]
 
-    def give(n):
-        j, bits = n // GROUP, n % GROUP
-        unit = unit_of(n)
+    def give(j, owner, t):
         return remote(
-            results.at[unit],
-            column_of(out, j),
-            o_send.at[j, bits],
-            o_got.at[j, bits],
-            base + flipped_by(member, bits),
-        )
-
-    def take(j, bits):
-        owner = flipped_by(member, bits)
-        at = pl.multiple_of((owner * SHARED + j) * HEAD_WIDTH, HEAD_WIDTH)
-        return remote(
-            results.at[j * GROUP],
-            out.at[:, pl.ds(at, HEAD_WIDTH)],
-            o_send.at[j, bits],
-            o_got.at[j, bits],
-            base + owner,
+            results.at[j * GROUP + t],
+            column_of(out, owner, j),
+            o_send.at[j, t],
+            o_got.at[j, owner],
+            base + t,
         )
 
     def hold(j):
         return pltpu.make_async_copy(
-            results.at[j * GROUP + member], column_of(out, j), own.at[3 + j]
+            results.at[j * GROUP + member], column_of(out, member, j), own.at[3 + j]
         )
 
-    def hand_out(n):
-        @pl.when(n % GROUP > 0)
+    def hand_out(unit):
+        j, t = unit // GROUP, unit % GROUP
+
+        @pl.when(t != member)
         def _():
-            give(n).start()
-
-        @pl.when(n % GROUP == 0)
+            give(j, member, t).start()
+
+        @pl.when(t == member)
         def _():
-            hold(n // GROUP).start()
-
-    def mix_step(n, carry):
-        mix_unit(unit_of(2 * n))
-        mix_unit(unit_of(2 * n + 1))
-
-        @pl.when(n > 0)
-        def _():
-            hand_out(2 * n - 2)
-            hand_out(2 * n - 1)
-
-        return carry
-
-    lax.fori_loop(0, units // 2, mix_step, 0)
-    hand_out(units - 2)
-    hand_out(units - 1)
-    for which in range(3):
-        for copy in near[which]:
-            copy.wait_send()
-    lax.fori_loop(0, groups, k_sent, 0)
-    lax.fori_loop(0, groups, v_sent, 0)
+            hold(j).start()
+
+    def q_ready(stage):
+        for i in range(each):
+            t = stage + stages * i
+
+            @pl.when(member == t)
+            def _():
+                stay[2].wait()
+
+            @pl.when(member != t)
+            def _():
+                near_q(t, t).wait_recv()
+
+    def between(far, first, count, total, work, after):
+        def piece(n, carry):
+            start, stop = n * total // count, (n + 1) * total // count
+
+            def inner(u, carry):
+                work(u)
+                return carry
+
+            lax.fori_loop(start, stop, inner, 0)
+            far(first + n)
+            if after is not None:
+
+                def later(u, carry):
+                    after(u)
+                    return carry
+
+                lax.fori_loop(start, stop, later, 0)
+            return carry
+
+        lax.fori_loop(0, count, piece, 0)
+
+    def job_of(kind, stage):
+        if kind == 0:
+            return in_stage, (lambda u: score_unit(unit_in(stage, u))), None
+
+        def mix(u):
+            mix_unit(unit_in(stage, 2 * u))
+            mix_unit(unit_in(stage, 2 * u + 1))
+
+        def send(u):
+            hand_out(unit_in(stage, 2 * u))
+            hand_out(unit_in(stage, 2 * u + 1))
+
+        return in_stage // 2, mix, send
+
+    phases = 2 * stages
+    jobs = [(kind, stage) for stage in range(stages) for kind in range(2)]
+    opening = min(3, phases - 1)
+    set_off(0)
+    for phase in range(phases):
+        stage, which = phase // 2, phase % 2
+        if phase + 1 < phases:
+            set_off(phase + 1)
+        far_step = (k_relay, v_relay)[which][1]
+
+        def far(n, far_step=far_step, stage=stage):
+            far_step(n // each + 1, stage + stages * (n % each))
+
+        now = []
+        while phase >= opening and len(now) < 2 and jobs and 2 * jobs[0][1] + jobs[0][0] < phase:
+            now.append(jobs.pop(0))
+        done = 0
+        for at, (kind, work_stage) in enumerate(now):
+            if kind == 0:
+                q_ready(work_stage)
+            share = steps * (at + 1) // len(now) - done
+            between(far, done, share, *job_of(kind, work_stage))
+            done += share
+        if not now:
+            between(far, 0, steps, 0, lambda u: None, None)
+        note(phase)
+    for kind, stage in jobs:
+        total, work, after = job_of(kind, stage)
+        if kind == 0:
+            q_ready(stage)
+
+        def last(n, carry, work=work, after=after):
+            work(n)
+            if after is not None:
+
+                @pl.when(n > 0)
+                def _():
+                    after(n - 1)
+
+            return carry
+
+        lax.fori_loop(0, total, last, 0)
+        if after is not None:
+            after(total - 1)
+    for bits in ORDER:
+        to = flipped(member, bits)
+        near_kv(0, member, to).wait_send()
+        near_kv(1, member, to).wait_send()
+        near_q(member, to).wait_send()
+    lax.fori_loop(0, groups, k_relay[2], 0)
+    lax.fori_loop(0, groups, v_relay[2], 0)
     for j in range(SHARED):
         hold(j).wait()
         for bits in ORDER:
-            give(j * GROUP + bits).wait_send()
-            take(j, bits).wait_recv()
+            other = flipped(member, bits)
+            give(j, member, other).wait_send()
+            give(j, other, other).wait_recv()
 
 
 def shards(queries, key_row_matrix, values, verticals, slashes, counts):
@@ -345,6 +403,7 @@
     units = SHARED * GROUP
     slots = 1 + verticals.shape[1] + slashes.shape[1]
     block = (BLOCK_TOKENS, HEAD_WIDTH)
+    seen = count if stages_for(lax.axis_size("seq")) > 1 else 1
     out = pl.pallas_call(
         functools.partial(kernel, groups),
         name="block_sparse_attention",
@@ -358,6 +417,8 @@
             pltpu.VMEM((units, slots, BLOCK_TOKENS, BLOCK_TOKENS), jnp.float32),
             pltpu.VMEM((units, BLOCK_TOKENS, BLOCK_TOKENS), jnp.float32),
             pltpu.VMEM((units,) + block, jnp.bfloat16),
+            pltpu.VMEM((seen,) + block, jnp.bfloat16),
+            pltpu.VMEM((seen,) + block, jnp.bfloat16),
             pltpu.SemaphoreType.DMA((3 + SHARED,)),
             pltpu.SemaphoreType.DMA((2, GROUP)),
             pltpu.SemaphoreType.DMA((2, GROUP)),

time: 63.1 us -> 68.2 us (1.081); the launches traced: 61.9 us -> 68 us
  Pallas kernels: 59.6 us -> 65.7 us
    pallas_call x1, Pallas kernels: 59.6 us -> 65.7 us  [shards(): pl.pallas_call(functools.partial(kernel, groups), name='block_sparse_atte...]
where the time goes in v2:
time: 68.2 us; the launch traced here: 68 us
  Pallas kernels  65.7 us (96%)
  local copies, waits for them, and re-layouts  2.29 us (3%)
    pallas_call x1, Pallas kernels, shards(): pl.pallas_call(functools.partial(kernel, groups), name='block_sparse_atte...  65.7 us
    unnamed x1, local copies, waits for them, and re-layouts  2.29 us

profile of v2, /device:TPU:5, one launch (start us, length us, event | category | flops | bytes accessed | tf_op | source)
XLA Modules:
  0.0 68.0 jit_solution(2247429003578744265)
XLA Ops:
  0.0 65.7 %block_sparse_attention.1 = bf16[128,4096]{1,0:T(8,128)(2,1)} custom-call(s32[6,32]{1,0:T(8,128)} %bitcast.11, s32[3,32]{1,0:T(4,128)} %bitcast.12, s32[2,32]{1,0:T(2,128)} %bitcast.13, bf16[128,4096]{1,0:T(8,128)(2,1)} %bitcast.8, bf16[128,1024]{1,0:T(8,128)(2,1)} %bitcast.9, bf16[128,1024]{1,0:T(8,128)(2,1)} %bitcast.10), custom_call_target="tpu_custom_call" | custom-call | tf_op jit(solution)/shard_map/block_sparse_attention/pallas_call | solution.py:407
  65.7 2.3 %copy.8 = bf16[1,128,4096]{2,1,0:T(8,128)(2,1)} copy(bf16[1,128,4096]{2,1,0:T(8,128)(2,1)} %bitcast.7) | data formatting | bytes 2097152

commit v3 on v2

--- a/solution.py
+++ b/solution.py
@@ -338,12 +338,13 @@
 
     phases = 2 * stages
     jobs = [(kind, stage) for stage in range(stages) for kind in range(2)]
-    opening = min(3, phases - 1)
-    set_off(0)
+    opening = min(4, phases - 1)
+    for phase in range(min(2, phases)):
+        set_off(phase)
     for phase in range(phases):
         stage, which = phase // 2, phase % 2
-        if phase + 1 < phases:
-            set_off(phase + 1)
+        if phase + 2 < phases:
+            set_off(phase + 2)
         far_step = (k_relay, v_relay)[which][1]
 
         def far(n, far_step=far_step, stage=stage):

time: 68.2 us -> 69 us (1.012)
  Pallas kernels: 65.7 us -> 66.5 us
    pallas_call x1, Pallas kernels: 65.7 us -> 66.5 us  [shards(): pl.pallas_call(functools.partial(kernel, groups), name='block_sparse_atte...]
where the time goes in v3:
time: 69 us; the launch traced here: 68.8 us
  Pallas kernels  66.5 us (96%)
  local copies, waits for them, and re-layouts  2.29 us (3%)
    pallas_call x1, Pallas kernels, shards(): pl.pallas_call(functools.partial(kernel, groups), name='block_sparse_atte...  66.5 us
    unnamed x1, local copies, waits for them, and re-layouts  2.29 us

profile of v3, /device:TPU:5, one launch (start us, length us, event | category | flops | bytes accessed | tf_op | source)
XLA Modules:
  0.0 68.8 jit_solution(12495089487443614050)
XLA Ops:
  0.0 66.5 %block_sparse_attention.1 = bf16[128,4096]{1,0:T(8,128)(2,1)} custom-call(s32[6,32]{1,0:T(8,128)} %bitcast.11, s32[3,32]{1,0:T(4,128)} %bitcast.12, s32[2,32]{1,0:T(2,128)} %bitcast.13, bf16[128,4096]{1,0:T(8,128)(2,1)} %bitcast.8, bf16[128,1024]{1,0:T(8,128)(2,1)} %bitcast.9, bf16[128,1024]{1,0:T(8,128)(2,1)} %bitcast.10), custom_call_target="tpu_custom_call" | custom-call | tf_op jit(solution)/shard_map/block_sparse_attention/pallas_call | solution.py:408
  66.5 2.3 %copy.8 = bf16[1,128,4096]{2,1,0:T(8,128)(2,1)} copy(bf16[1,128,4096]{2,1,0:T(8,128)(2,1)} %bitcast.7) | data formatting | bytes 2097152
